TPU v7x, 32 devices: a whole 2x2x4 slice. The times are simulated.
32 devices in a mesh: row: 8 (over z, x), col: 4 (over y, core).
Axes of the slice: x: 2, y: 2, z: 4, core: 2. Of those that a mesh axis runs over, the one named last changes fastest.
Arguments:
- block_cost: bfloat16 [128, 16, 256, 256], P('row', 'col'), may hold values from 0 to 15, as said below
- candidates: int32 [128, 16], P('row', 'col'), may hold values from 0 to 31, all different within a row
- source_logmass: float32 [128, 256], P('row'), may hold values from -4 to 4
- target_logmass: float32 [32, 256], replicated, may hold values from -4 to 4
Outputs:
- source_potential: float32 [128, 256], P('row')
- target_potential: float32 [32, 256], replicated
Inputs may be any that keep to these rules, and one draw needn't show every extreme that they name: Each row of candidates names 16 distinct target blocks, and every target block is named by some row. `block_cost`: costs are nonnegative.
All inputs are finite; a program needn't handle non-finite values.
Results may differ from a plain program's by a relative error of at most 0.0003.
Values sent between devices are 32-bit elements; how exact they have to be, the bound alone decides.
No kernel may reach another device: no remote copies, remote signals or barrier semaphores. Data moves between devices by JAX's collectives and lax.ppermute only.
A program may use at most 256 MiB of HBM per device.

v0:
```python
import jax
import jax.numpy as jnp
from jax import lax
from jax.sharding import PartitionSpec as P

ITERS = 2
EPS = 0.05
LOWEST = -1e30


def per_device(block_cost, candidates, source_logmass, target_logmass):
    target_pot = jnp.zeros(target_logmass.shape, jnp.float32)
    source_pot = jnp.zeros(source_logmass.shape, jnp.float32)
    block_size = block_cost.shape[3]
    flat_ids = candidates.reshape(-1)
    for step_index in range(ITERS):
        nearby = target_pot[candidates]
        scores = (nearby[:, :, None, :] - block_cost.astype(jnp.float32)) / EPS
        highest = jnp.max(scores, axis=(1, 3))
        totals = jnp.sum(jnp.exp(scores - highest[:, None, :, None]), axis=(1, 3))
        row_peak = lax.pmax(highest, "col")
        totals = lax.psum(totals * jnp.exp(highest - row_peak), "col")
        highest = row_peak
        source_pot = EPS * source_logmass - EPS * (highest + jnp.log(totals))
        col_scores = (source_pot[:, None, :, None] - block_cost.astype(jnp.float32)) / EPS
        col_high = jnp.max(col_scores, axis=2).reshape(-1, block_size)
        col_total = jnp.sum(
            jnp.exp(col_scores - jnp.max(col_scores, axis=2)[:, :, None, :]), axis=2
        ).reshape(-1, block_size)
        peaks = jnp.full(target_logmass.shape, LOWEST, jnp.float32).at[flat_ids].max(col_high)
        masses = (
            jnp.zeros(target_logmass.shape, jnp.float32)
            .at[flat_ids]
            .add(col_total * jnp.exp(col_high - peaks[flat_ids]))
        )
        all_peaks = lax.pmax(peaks, ("row", "col"))
        masses = lax.psum(masses * jnp.exp(peaks - all_peaks), ("row", "col"))
        target_pot = EPS * target_logmass - EPS * (all_peaks + jnp.log(masses))
    return (source_pot, target_pot)


def solution(mesh):
    return jax.shard_map(
        per_device,
        mesh=mesh,
        in_specs=(P("row", "col", None, None), P("row", "col"), P("row", None), P()),
        out_specs=(P("row", None), P()),
        check_vma=False,
    )
```

profile of v0, /device:TPU:0, one launch (start us, length us, event | category | flops | bytes accessed | tf_op | source)
XLA Modules:
  0.0 260.1 jit_solution(773136347404599062)
XLA Ops:
  0.6 0.7 compare_select_fusion
  1.3 0.1 copy.9
  1.4 0.1 reshape.62
  1.5 0.8 copy.8
  2.3 0.1 reshape.55
  2.4 0.7 gather_fusion
  3.1 0.0 copy-start
  3.1 0.0 copy-start.3
  3.1 5.8 %fusion.2 = f32[16,256]{1,0:T(8,128)S(1)} fusion(bf16[16,4,256,256]{3,2,1,0:T(8,128)(2,1)} %param.4, f32[16,4,256]{2,1,0:T(4,128)S(1)} %reshape.61), kind=kLoop, calls=%fused_computation.14 | loop fusion | flops 16773120 | bytes 8470528 | tf_op jit(solution)/shard_map/reduce_max | solution.py:19
  8.9 0.0 copy-done
  8.9 4.6 %fusion.4 = f32[16,256]{1,0:T(8,128)S(1)} fusion(bf16[16,4,256,256]{3,2,1,0:T(8,128)(2,1)S(1)} %copy-done, f32[16,256]{1,0:T(8,128)S(1)} %fusion.2, f32[16,4,256]{2,1,0:T(4,128)S(1)} %reshape.61), kind=kLoop, calls=%fused_computation.16 | loop fusion | flops 20967424 | bytes 8486912 | tf_op jit(solution)/shard_map/reduce_sum | solution.py:20
  13.6 12.7 %pmax.28 = f32[16,256]{1,0:T(8,128)S(1)} all-reduce(f32[16,256]{1,0:T(8,128)S(1)} %fusion.2), channel_id=1, replica_groups=mesh['row'=8,'col'=4] {'col'}, use_global_device_ids=true, to_apply=%region_1.0 | all-reduce | flops 4096 | bytes 32768 | tf_op jit(solution)/shard_map/pmax | solution.py:21
  26.3 10.1 %psum.28 = f32[16,256]{1,0:T(8,128)S(1)} all-reduce(f32[16,256]{1,0:T(8,128)S(1)} %exponential_multiply_fusion.3), channel_id=1, replica_groups=mesh['row'=8,'col'=4] {'col'}, use_global_device_ids=true, to_apply=%region_3.0 | all-reduce | flops 4096 | bytes 32768 | tf_op jit(solution)/shard_map/psum | solution.py:22
  36.4 0.0 copy-done.3
  36.4 0.0 copy-start.2
  36.4 5.3 %fusion.7 = f32[16,4,256]{2,1,0:T(4,128)S(1)} fusion(bf16[16,4,256,256]{3,2,1,0:T(8,128)(2,1)} %param.4, f32[16,256]{1,0:T(8,128)S(1)} %multiply_subtract_fusion.3), kind=kLoop, calls=%fused_computation.19 | loop fusion | flops 16760832 | bytes 8470528 | tf_op jit(solution)/shard_map/reduce_max | solution.py:26
  41.7 6.6 %fusion.9 = f32[16,4,256]{2,1,0:T(4,128)S(1)} fusion(bf16[16,4,256,256]{3,2,1,0:T(8,128)(2,1)} %param.4, f32[16,4,256]{2,1,0:T(4,128)S(1)} %fusion.7, f32[16,256]{1,0:T(8,128)S(1)} %multiply_subtract_fusion.3), kind=kLoop, calls=%fused_computation.21 | loop fusion | flops 20955136 | bytes 8536064 | tf_op jit(solution)/shard_map/reduce_sum | solution.py:27
  48.4 0.9 scatter_custom_fusion
  49.4 1.1 scatter_custom_fusion.1
  50.5 39.7 %pmax.29 = f32[32,256]{1,0:T(8,128)S(1)} all-reduce(f32[32,256]{1,0:T(8,128)S(1)} %scatter_custom_fusion), channel_id=1, replica_groups=mesh['row'=8,'col'=4] {'row','col'}, use_global_device_ids=true, to_apply=%region_6.0 | all-reduce | flops 8192 | bytes 65536 | tf_op jit(solution)/shard_map/pmax | solution.py:36
  90.3 41.3 %psum.29 = f32[32,256]{1,0:T(8,128)S(1)} all-reduce(f32[32,256]{1,0:T(8,128)S(1)} %exponential_multiply_fusion.1), channel_id=1, replica_groups=mesh['row'=8,'col'=4] {'row','col'}, use_global_device_ids=true, to_apply=%region_9.0 | all-reduce | flops 8192 | bytes 65536 | tf_op jit(solution)/shard_map/psum | solution.py:37
  131.5 0.0 copy-done.2
  131.6 0.7 gather_fusion.1
  132.3 5.7 %fusion.12 = f32[16,256]{1,0:T(8,128)S(1)} fusion(bf16[16,4,256,256]{3,2,1,0:T(8,128)(2,1)} %param.4, f32[16,4,256]{2,1,0:T(4,128)S(1)} %reshape.77), kind=kLoop, calls=%fused_computation.24 | loop fusion | flops 16773120 | bytes 8470528 | tf_op jit(solution)/shard_map/reduce_max | solution.py:19
  137.9 6.7 %fusion.14 = f32[16,256]{1,0:T(8,128)S(1)} fusion(bf16[16,4,256,256]{3,2,1,0:T(8,128)(2,1)} %param.4, f32[16,256]{1,0:T(8,128)S(1)} %fusion.12, f32[16,4,256]{2,1,0:T(4,128)S(1)} %reshape.77), kind=kLoop, calls=%fused_computation.26 | loop fusion | flops 20967424 | bytes 8486912 | tf_op jit(solution)/shard_map/reduce_sum | solution.py:20
  144.6 10.2 %pmax.30 = f32[16,256]{1,0:T(8,128)S(1)} all-reduce(f32[16,256]{1,0:T(8,128)S(1)} %fusion.12), channel_id=1, replica_groups=mesh['row'=8,'col'=4] {'col'}, use_global_device_ids=true, to_apply=%region_11.0 | all-reduce | flops 4096 | bytes 32768 | tf_op jit(solution)/shard_map/pmax | solution.py:21
  154.8 10.1 %psum.30 = f32[16,256]{1,0:T(8,128)S(1)} all-reduce(f32[16,256]{1,0:T(8,128)S(1)} %exponential_multiply_fusion.2), channel_id=1, replica_groups=mesh['row'=8,'col'=4] {'col'}, use_global_device_ids=true, to_apply=%region_13.0 | all-reduce | flops 4096 | bytes 32768 | tf_op jit(solution)/shard_map/psum | solution.py:22
  164.9 0.0 copy-start.1
  164.9 5.3 %fusion.17 = f32[16,4,256]{2,1,0:T(4,128)S(1)} fusion(bf16[16,4,256,256]{3,2,1,0:T(8,128)(2,1)} %param.4, f32[16,256]{1,0:T(8,128)S(1)} %multiply_subtract_fusion.2), kind=kLoop, calls=%fused_computation.29 | loop fusion | flops 16760832 | bytes 8470528 | tf_op jit(solution)/shard_map/reduce_max | solution.py:26
  170.3 6.6 %fusion.19 = f32[16,4,256]{2,1,0:T(4,128)S(1)} fusion(bf16[16,4,256,256]{3,2,1,0:T(8,128)(2,1)} %param.4, f32[16,4,256]{2,1,0:T(4,128)S(1)} %fusion.17, f32[16,256]{1,0:T(8,128)S(1)} %multiply_subtract_fusion.2), kind=kLoop, calls=%fused_computation.31 | loop fusion | flops 20955136 | bytes 8536064 | tf_op jit(solution)/shard_map/reduce_sum | solution.py:27
  176.9 0.0 copy-done.1
  176.9 0.9 scatter_custom_fusion.2
  177.9 1.1 scatter_custom_fusion.3
  179.0 39.2 %pmax.31 = f32[32,256]{1,0:T(8,128)S(1)} all-reduce(f32[32,256]{1,0:T(8,128)S(1)} %scatter_custom_fusion.2), channel_id=1, replica_groups=mesh['row'=8,'col'=4] {'row','col'}, use_global_device_ids=true, to_apply=%region_16.0 | all-reduce | flops 8192 | bytes 65536 | tf_op jit(solution)/shard_map/pmax | solution.py:36
  218.2 41.2 %psum.31 = f32[32,256]{1,0:T(8,128)S(1)} all-reduce(f32[32,256]{1,0:T(8,128)S(1)} %exponential_multiply_fusion), channel_id=1, replica_groups=mesh['row'=8,'col'=4] {'row','col'}, use_global_device_ids=true, to_apply=%region_19.0 | all-reduce | flops 8192 | bytes 65536 | tf_op jit(solution)/shard_map/psum | solution.py:37
  259.5 0.6 multiply_subtract_fusion
  (17 shorter events, 0.3 us)
Async XLA Ops:
  3.1 5.8 %copy-start = (bf16[16,4,256,256]{3,2,1,0:T(8,128)(2,1)S(1)}, bf16[16,4,256,256]{3,2,1,0:T(8,128)(2,1)}, u32[]{:S(2)}) copy-start(bf16[16,4,256,256]{3,2,1,0:T(8,128)(2,1)} %param.4) | copy-start | bytes 25165828
  3.1 33.3 %copy-start.3 = (f32[16,256]{1,0:T(8,128)S(1)}, f32[16,256]{1,0:T(8,128)}, u32[]{:S(2)}) copy-start(f32[16,256]{1,0:T(8,128)} %param.6) | copy-start | bytes 49156
  36.4 95.1 %copy-start.2 = (f32[32,256]{1,0:T(8,128)S(1)}, f32[32,256]{1,0:T(8,128)}, u32[]{:S(2)}) copy-start(f32[32,256]{1,0:T(8,128)} %param.7) | copy-start | bytes 98308
  164.9 12.0 %copy-start.1 = (f32[16,256]{1,0:T(8,128)}, f32[16,256]{1,0:T(8,128)S(1)}, u32[]{:S(2)}) copy-start(f32[16,256]{1,0:T(8,128)S(1)} %multiply_subtract_fusion.2) | copy-start | bytes 49156
where the time goes:
time: 261 us; the launch traced here: 260 us
  blocking collectives  204 us (78%)
  other arithmetic  52.2 us (20%)
    psum x2, blocking collectives, per_device(): masses = lax.psum(masses * jnp.exp(peaks - all_peaks), ('row', 'col'))  82.5 us
    pmax x2, blocking collectives, per_device(): all_peaks = lax.pmax(peaks, ('row', 'col'))  78.9 us
    pmax x2, blocking collectives, per_device(): row_peak = lax.pmax(highest, 'col')  22.9 us
    psum x2, blocking collectives, per_device(): totals = lax.psum(totals * jnp.exp(highest - row_peak), 'col')  20.2 us
    reduce_sum x2, other arithmetic, per_device(): jnp.sum(jnp.exp(col_scores - jnp.max(col_scores, axis=2)[:, :, None, :]),...  13.2 us
    reduce_max x2, other arithmetic, per_device(): highest = jnp.max(scores, axis=(1, 3))  11.5 us
    reduce_sum x2, other arithmetic, per_device(): totals = jnp.sum(jnp.exp(scores - highest[:, None, :, None]), axis=(1, 3))  11.3 us
    reduce_max x2, other arithmetic, per_device(): col_high = jnp.max(col_scores, axis=2).reshape(-1, block_size)  10.6 us

commit v1 on v0

--- a/solution.py
+++ b/solution.py
@@ -34,7 +34,7 @@
             .add(col_total * jnp.exp(col_high - peaks[flat_ids]))
         )
         all_peaks = lax.pmax(peaks, ("row", "col"))
-        masses = lax.psum(masses * jnp.exp(peaks - all_peaks), ("row", "col"))
+        masses = lax.psum(lax.psum(masses * jnp.exp(peaks - all_peaks), "col"), "row")
         target_pot = EPS * target_logmass - EPS * (all_peaks + jnp.log(masses))
     return (source_pot, target_pot)
 

time: 261 us -> 270 us (1.034)
  blocking collectives: 204 us -> 214 us
    psum x2 -> x4, blocking collectives: 82.5 us -> 94.2 us  [the longest x2 71.8 us: per_device(): lax.psum(lax.psum(masses * jnp.exp(peaks - all_peaks), 'col'), 'row')]
where the time goes in v1:
time: 270 us
  blocking collectives  214 us (79%)
  other arithmetic  52.2 us (19%)
    pmax x2, blocking collectives, per_device(): all_peaks = lax.pmax(peaks, ('row', 'col'))  76.8 us
    psum x2, blocking collectives, per_device(): lax.psum(lax.psum(masses * jnp.exp(peaks - all_peaks), 'col'), 'row')  71.8 us
    pmax x2, blocking collectives, per_device(): row_peak = lax.pmax(highest, 'col')  22.8 us
    psum x2, blocking collectives, per_device(): lax.psum(masses * jnp.exp(peaks - all_peaks), 'col')  22.4 us
    psum x2, blocking collectives, per_device(): totals = lax.psum(totals * jnp.exp(highest - row_peak), 'col')  20.2 us
    reduce_sum x2, other arithmetic, per_device(): jnp.sum(jnp.exp(col_scores - jnp.max(col_scores, axis=2)[:, :, None, :]),...  13.2 us
    reduce_max x2, other arithmetic, per_device(): highest = jnp.max(scores, axis=(1, 3))  11.5 us
    reduce_sum x2, other arithmetic, per_device(): totals = jnp.sum(jnp.exp(scores - highest[:, None, :, None]), axis=(1, 3))  11.3 us

profile of v1, /device:TPU:0, one launch (start us, length us, event | category | flops | bytes accessed | tf_op | source)
XLA Modules:
  0.0 269.6 jit_solution(13488842983107419989)
XLA Ops:
  0.6 0.7 compare_select_fusion
  1.3 0.1 copy.9
  1.4 0.1 reshape.62
  1.5 0.8 copy.8
  2.3 0.1 reshape.55
  2.4 0.7 gather_fusion
  3.1 0.0 copy-start
  3.1 0.0 copy-start.3
  3.1 5.8 %fusion.2 = f32[16,256]{1,0:T(8,128)S(1)} fusion(bf16[16,4,256,256]{3,2,1,0:T(8,128)(2,1)} %param.4, f32[16,4,256]{2,1,0:T(4,128)S(1)} %reshape.61), kind=kLoop, calls=%fused_computation.14 | loop fusion | flops 16773120 | bytes 8470528 | tf_op jit(solution)/shard_map/reduce_max | solution.py:19
  8.9 0.0 copy-done
  8.9 4.6 %fusion.4 = f32[16,256]{1,0:T(8,128)S(1)} fusion(bf16[16,4,256,256]{3,2,1,0:T(8,128)(2,1)S(1)} %copy-done, f32[16,256]{1,0:T(8,128)S(1)} %fusion.2, f32[16,4,256]{2,1,0:T(4,128)S(1)} %reshape.61), kind=kLoop, calls=%fused_computation.16 | loop fusion | flops 20967424 | bytes 8486912 | tf_op jit(solution)/shard_map/reduce_sum | solution.py:20
  13.6 12.7 %pmax.28 = f32[16,256]{1,0:T(8,128)S(1)} all-reduce(f32[16,256]{1,0:T(8,128)S(1)} %fusion.2), channel_id=1, replica_groups=mesh['row'=8,'col'=4] {'col'}, use_global_device_ids=true, to_apply=%region_1.0 | all-reduce | flops 4096 | bytes 32768 | tf_op jit(solution)/shard_map/pmax | solution.py:21
  26.3 10.1 %psum.42 = f32[16,256]{1,0:T(8,128)S(1)} all-reduce(f32[16,256]{1,0:T(8,128)S(1)} %exponential_multiply_fusion.3), channel_id=1, replica_groups=mesh['row'=8,'col'=4] {'col'}, use_global_device_ids=true, to_apply=%region_3.0 | all-reduce | flops 4096 | bytes 32768 | tf_op jit(solution)/shard_map/psum | solution.py:22
  36.4 0.0 copy-done.3
  36.4 0.0 copy-start.2
  36.4 5.3 %fusion.7 = f32[16,4,256]{2,1,0:T(4,128)S(1)} fusion(bf16[16,4,256,256]{3,2,1,0:T(8,128)(2,1)} %param.4, f32[16,256]{1,0:T(8,128)S(1)} %multiply_subtract_fusion.3), kind=kLoop, calls=%fused_computation.19 | loop fusion | flops 16760832 | bytes 8470528 | tf_op jit(solution)/shard_map/reduce_max | solution.py:26
  41.7 6.6 %fusion.9 = f32[16,4,256]{2,1,0:T(4,128)S(1)} fusion(bf16[16,4,256,256]{3,2,1,0:T(8,128)(2,1)} %param.4, f32[16,4,256]{2,1,0:T(4,128)S(1)} %fusion.7, f32[16,256]{1,0:T(8,128)S(1)} %multiply_subtract_fusion.3), kind=kLoop, calls=%fused_computation.21 | loop fusion | flops 20955136 | bytes 8536064 | tf_op jit(solution)/shard_map/reduce_sum | solution.py:27
  48.4 0.9 scatter_custom_fusion
  49.4 1.1 scatter_custom_fusion.1
  50.5 39.7 %pmax.29 = f32[32,256]{1,0:T(8,128)S(1)} all-reduce(f32[32,256]{1,0:T(8,128)S(1)} %scatter_custom_fusion), channel_id=1, replica_groups=mesh['row'=8,'col'=4] {'row','col'}, use_global_device_ids=true, to_apply=%region_6.0 | all-reduce | flops 8192 | bytes 65536 | tf_op jit(solution)/shard_map/pmax | solution.py:36
  90.3 11.2 %psum.43 = f32[32,256]{1,0:T(8,128)S(1)} all-reduce(f32[32,256]{1,0:T(8,128)S(1)} %exponential_multiply_fusion.1), channel_id=1, replica_groups=mesh['row'=8,'col'=4] {'col'}, use_global_device_ids=true, to_apply=%region_9.0 | all-reduce | flops 8192 | bytes 65536 | tf_op jit(solution)/shard_map/psum | solution.py:37
  101.5 35.9 %psum.44 = f32[32,256]{1,0:T(8,128)S(1)} all-reduce(f32[32,256]{1,0:T(8,128)S(1)} %psum.43), channel_id=1, replica_groups=mesh['row'=8,'col'=4] {'row'}, use_global_device_ids=true, to_apply=%region_10.0 | all-reduce | flops 8192 | bytes 65536 | tf_op jit(solution)/shard_map/psum | solution.py:37
  137.3 0.0 copy-done.2
  137.3 0.7 gather_fusion.1
  138.0 5.7 %fusion.12 = f32[16,256]{1,0:T(8,128)S(1)} fusion(bf16[16,4,256,256]{3,2,1,0:T(8,128)(2,1)} %param.4, f32[16,4,256]{2,1,0:T(4,128)S(1)} %reshape.77), kind=kLoop, calls=%fused_computation.24 | loop fusion | flops 16773120 | bytes 8470528 | tf_op jit(solution)/shard_map/reduce_max | solution.py:19
  143.7 6.7 %fusion.14 = f32[16,256]{1,0:T(8,128)S(1)} fusion(bf16[16,4,256,256]{3,2,1,0:T(8,128)(2,1)} %param.4, f32[16,256]{1,0:T(8,128)S(1)} %fusion.12, f32[16,4,256]{2,1,0:T(4,128)S(1)} %reshape.77), kind=kLoop, calls=%fused_computation.26 | loop fusion | flops 20967424 | bytes 8486912 | tf_op jit(solution)/shard_map/reduce_sum | solution.py:20
  150.4 10.1 %pmax.30 = f32[16,256]{1,0:T(8,128)S(1)} all-reduce(f32[16,256]{1,0:T(8,128)S(1)} %fusion.12), channel_id=1, replica_groups=mesh['row'=8,'col'=4] {'col'}, use_global_device_ids=true, to_apply=%region_12.0 | all-reduce | flops 4096 | bytes 32768 | tf_op jit(solution)/shard_map/pmax | solution.py:21
  160.5 10.1 %psum.45 = f32[16,256]{1,0:T(8,128)S(1)} all-reduce(f32[16,256]{1,0:T(8,128)S(1)} %exponential_multiply_fusion.2), channel_id=1, replica_groups=mesh['row'=8,'col'=4] {'col'}, use_global_device_ids=true, to_apply=%region_14.0 | all-reduce | flops 4096 | bytes 32768 | tf_op jit(solution)/shard_map/psum | solution.py:22
  170.6 0.0 copy-start.1
  170.6 5.3 %fusion.17 = f32[16,4,256]{2,1,0:T(4,128)S(1)} fusion(bf16[16,4,256,256]{3,2,1,0:T(8,128)(2,1)} %param.4, f32[16,256]{1,0:T(8,128)S(1)} %multiply_subtract_fusion.2), kind=kLoop, calls=%fused_computation.29 | loop fusion | flops 16760832 | bytes 8470528 | tf_op jit(solution)/shard_map/reduce_max | solution.py:26
  176.0 6.6 %fusion.19 = f32[16,4,256]{2,1,0:T(4,128)S(1)} fusion(bf16[16,4,256,256]{3,2,1,0:T(8,128)(2,1)} %param.4, f32[16,4,256]{2,1,0:T(4,128)S(1)} %fusion.17, f32[16,256]{1,0:T(8,128)S(1)} %multiply_subtract_fusion.2), kind=kLoop, calls=%fused_computation.31 | loop fusion | flops 20955136 | bytes 8536064 | tf_op jit(solution)/shard_map/reduce_sum | solution.py:27
  182.6 0.0 copy-done.1
  182.7 0.9 scatter_custom_fusion.2
  183.6 1.1 scatter_custom_fusion.3
  184.7 37.1 %pmax.31 = f32[32,256]{1,0:T(8,128)S(1)} all-reduce(f32[32,256]{1,0:T(8,128)S(1)} %scatter_custom_fusion.2), channel_id=1, replica_groups=mesh['row'=8,'col'=4] {'row','col'}, use_global_device_ids=true, to_apply=%region_17.0 | all-reduce | flops 8192 | bytes 65536 | tf_op jit(solution)/shard_map/pmax | solution.py:36
  221.8 11.2 %psum.46 = f32[32,256]{1,0:T(8,128)S(1)} all-reduce(f32[32,256]{1,0:T(8,128)S(1)} %exponential_multiply_fusion), channel_id=1, replica_groups=mesh['row'=8,'col'=4] {'col'}, use_global_device_ids=true, to_apply=%region_20.0 | all-reduce | flops 8192 | bytes 65536 | tf_op jit(solution)/shard_map/psum | solution.py:37
  233.0 35.9 %psum.47 = f32[32,256]{1,0:T(8,128)S(1)} all-reduce(f32[32,256]{1,0:T(8,128)S(1)} %psum.46), channel_id=1, replica_groups=mesh['row'=8,'col'=4] {'row'}, use_global_device_ids=true, to_apply=%region_21.0 | all-reduce | flops 8192 | bytes 65536 | tf_op jit(solution)/shard_map/psum | solution.py:37
  269.0 0.6 multiply_subtract_fusion
  (17 shorter events, 0.3 us)
Async XLA Ops:
  3.1 5.8 %copy-start = (bf16[16,4,256,256]{3,2,1,0:T(8,128)(2,1)S(1)}, bf16[16,4,256,256]{3,2,1,0:T(8,128)(2,1)}, u32[]{:S(2)}) copy-start(bf16[16,4,256,256]{3,2,1,0:T(8,128)(2,1)} %param.4) | copy-start | bytes 25165828
  3.1 33.3 %copy-start.3 = (f32[16,256]{1,0:T(8,128)S(1)}, f32[16,256]{1,0:T(8,128)}, u32[]{:S(2)}) copy-start(f32[16,256]{1,0:T(8,128)} %param.6) | copy-start | bytes 49156
  36.4 100.9 %copy-start.2 = (f32[32,256]{1,0:T(8,128)S(1)}, f32[32,256]{1,0:T(8,128)}, u32[]{:S(2)}) copy-start(f32[32,256]{1,0:T(8,128)} %param.7) | copy-start | bytes 98308
  170.6 12.0 %copy-start.1 = (f32[16,256]{1,0:T(8,128)}, f32[16,256]{1,0:T(8,128)S(1)}, u32[]{:S(2)}) copy-start(f32[16,256]{1,0:T(8,128)S(1)} %multiply_subtract_fusion.2) | copy-start | bytes 49156
